TPU v7x, 32 devices: a whole 2x2x4 slice. The times are simulated.
32 devices in a mesh: parts: 2 (over x), row: 8 (over z, core), col: 2 (over y).
Axes of the slice: x: 2, y: 2, z: 4, core: 2. Of those that a mesh axis runs over, the one named last changes fastest.
Arguments:
- pair_features_map: bfloat16 [64, 1024, 512], P(None, ('parts', 'row'), 'col'), parts along dimension 1, may hold values from -6 to 6
- labels: int32 [1024, 512], P(('parts', 'row', 'col')), parts along dimension 0, may hold values from 0 to 36, as said below
- lengths: int32 [2], P('parts'), parts along dimension 0, may hold values from 256 to 512
- conv_weight: bfloat16 [3, 3, 64, 64], replicated, may hold values from -0.25 to 0.25
- conv_bias: float32 [64], replicated, may hold values from -3 to 3
- head_weight: bfloat16 [37, 64], replicated, may hold values from -2.390625 to 2.390625
- head_bias: float32 [37], replicated, may hold values from -4 to 4
Outputs:
- pair_gradient: bfloat16 [64, 1024, 512], P(None, ('parts', 'row'), 'col'), parts along dimension 1
- grad_conv_weight: float32 [6, 3, 64, 64], P('parts'), parts along dimension 0
- grad_conv_bias: float32 [128], P('parts'), parts along dimension 0
- grad_head_weight: float32 [74, 64], P('parts'), parts along dimension 0
- grad_head_bias: float32 [74], P('parts'), parts along dimension 0
- loss: float32 [2], P('parts'), parts along dimension 0
There are 2 independent parts, one for each index of `parts`. A program takes and returns all parts, laid end to end along the dimension named above; an argument that names none is the same for every part. Nothing has to cross between parts.
Inputs may be any that keep to these rules, and one draw needn't show every extreme that they name: labels[i, j] equals labels[j, i] for every pair.
All inputs are finite; a program needn't handle non-finite values.
Results may differ from a plain program's by a relative error of at most 0.0067.
Values may be sent and summed in bfloat16 or wider, within the bound.
No kernel may reach another device: no remote copies, remote signals or barrier semaphores. Data moves between devices by JAX's collectives and lax.ppermute only.
A program may use at most 128 MiB of HBM per device.

v0:
```python
import jax
import jax.numpy as jnp
from jax import lax
from jax.sharding import PartitionSpec as P

DILATION_STEP = 4


def with_halo(cells, sides, width):
    for axis, dim in sides:
        count = lax.axis_size(axis)
        ends = count - 1
        head = lax.slice_in_dim(cells, 0, width, axis=dim)
        tail = lax.slice_in_dim(cells, cells.shape[dim] - width, cells.shape[dim], axis=dim)
        cells = jnp.concatenate(
            [
                lax.ppermute(tail, axis, [(i, (i + 1) % count) for i in range(ends)]),
                cells,
                lax.ppermute(head, axis, [((i + 1) % count, i) for i in range(ends)]),
            ],
            axis=dim,
        )
    return cells


def tile_to_band(field):
    channels, patch_rows, patch_columns = field.shape
    width = lax.axis_size("col")
    split = field.reshape(channels, width, patch_rows // width, patch_columns)
    moved = lax.all_to_all(split, "col", split_axis=1, concat_axis=3, tiled=True)
    return moved.reshape(channels, patch_rows // width, width * patch_columns)


def band_to_tile(field):
    channels, band_rows, length_cols = field.shape
    width = lax.axis_size("col")
    split = field.reshape(channels, band_rows, width, length_cols // width)
    moved = lax.all_to_all(split, "col", split_axis=2, concat_axis=1, tiled=True)
    return moved.reshape(channels, width * band_rows, length_cols // width)


def reorder_back(moved, channels, band_rows, length_cols):
    return jnp.transpose(moved, (0, 3, 2, 1)).reshape(channels, band_rows, length_cols)


def mirror_features(field):
    channels, band_rows, length_cols = field.shape
    bands = lax.axis_size(("row", "col"))
    blocks = field.reshape(channels, band_rows, bands, band_rows)
    moved = lax.all_to_all(blocks, ("row", "col"), split_axis=2, concat_axis=2, tiled=True)
    return reorder_back(moved, channels, band_rows, length_cols)


def per_device(pair_features_map, labels, lengths, conv_weight, conv_bias, head_weight, head_bias):
    channels, patch_rows, patch_columns = pair_features_map.shape
    nbins = head_weight.shape[0]
    bordered_input = with_halo(pair_features_map, (("row", 1), ("col", 2)), DILATION_STEP)
    before_activation = (
        jnp.zeros((channels, patch_rows, patch_columns), jnp.float32) + conv_bias[:, None, None]
    )
    for offset_row in range(3):
        for offset_column in range(3):
            sliding_patch = bordered_input[
                :,
                DILATION_STEP * offset_row : DILATION_STEP * offset_row + patch_rows,
                DILATION_STEP * offset_column : DILATION_STEP * offset_column + patch_columns,
            ]
            before_activation = before_activation + jnp.einsum(
                "oc,cij->oij",
                conv_weight[offset_row, offset_column],
                sliding_patch,
                preferred_element_type=jnp.float32,
            )
    hidden_tile = jnp.where(
        before_activation > 0, before_activation, jnp.expm1(jnp.minimum(before_activation, 0.0))
    ).astype(jnp.bfloat16)
    hidden = tile_to_band(hidden_tile)
    band_rows, length_cols = (hidden.shape[1], hidden.shape[2])
    hidden_mirror = mirror_features(hidden)
    direct = jnp.einsum("kc,cij->kij", head_weight, hidden, preferred_element_type=jnp.float32)
    opposite = jnp.einsum(
        "kc,cij->kij", head_weight, hidden_mirror, preferred_element_type=jnp.float32
    )
    logits = 0.5 * (direct + opposite) + head_bias[:, None, None]
    band = lax.axis_index(("row", "col"))
    row_ids = band * band_rows + lax.broadcasted_iota(jnp.int32, (band_rows, length_cols), 0)
    col_ids = lax.broadcasted_iota(jnp.int32, (band_rows, length_cols), 1)
    extent = lengths[0]
    valid = ((row_ids < extent) & (col_ids < extent)).astype(jnp.float32)
    count = (extent * extent).astype(jnp.float32)
    onehot = (lax.broadcasted_iota(jnp.int32, (nbins, 1, 1), 0) == labels[None]).astype(jnp.float32)
    lse = jnp.log(jnp.sum(jnp.exp(logits), axis=0))
    picked = jnp.sum(onehot * logits, axis=0)
    loss_local = jnp.sum(valid * (lse - picked))
    dlogits = (valid[None] * (jnp.exp(logits - lse[None]) - onehot) / count).astype(jnp.bfloat16)
    head_grad = jnp.einsum("kij,cij->kc", dlogits, hidden, preferred_element_type=jnp.float32)
    head_bias_grad = jnp.sum(dlogits.astype(jnp.float32), axis=(1, 2))
    tile_grad = band_to_tile(dlogits)
    back = jnp.einsum("kc,kij->cij", head_weight, tile_grad, preferred_element_type=jnp.float32)
    slope = jnp.where(before_activation > 0, 1.0, jnp.exp(jnp.minimum(before_activation, 0.0)))
    preact_gradient = (back * slope).astype(jnp.bfloat16)
    preact_gradient_bordered = with_halo(preact_gradient, (("row", 1), ("col", 2)), DILATION_STEP)
    grad_field = jnp.zeros((channels, patch_rows, patch_columns), jnp.float32)
    tap_rows = []
    for offset_row in range(3):
        tap_cols = []
        for offset_column in range(3):
            sliding_patch = bordered_input[
                :,
                DILATION_STEP * offset_row : DILATION_STEP * offset_row + patch_rows,
                DILATION_STEP * offset_column : DILATION_STEP * offset_column + patch_columns,
            ]
            tap_cols.append(
                jnp.einsum(
                    "oij,cij->oc",
                    preact_gradient,
                    sliding_patch,
                    preferred_element_type=jnp.float32,
                )
            )
            row_begin = DILATION_STEP * (2 - offset_row)
            column_begin = DILATION_STEP * (2 - offset_column)
            source = preact_gradient_bordered[
                :, row_begin : row_begin + patch_rows, column_begin : column_begin + patch_columns
            ]
            grad_field = grad_field + jnp.einsum(
                "oc,oij->cij",
                conv_weight[offset_row, offset_column],
                source,
                preferred_element_type=jnp.float32,
            )
        tap_rows.append(jnp.stack(tap_cols))
    conv_grad = jnp.stack(tap_rows)
    conv_bias_grad = jnp.sum(preact_gradient.astype(jnp.float32), axis=(1, 2))
    conv_grad, conv_bias_grad, head_grad, head_bias_grad, loss_total = lax.psum(
        (conv_grad, conv_bias_grad, head_grad, head_bias_grad, loss_local), ("row", "col")
    )
    loss = (loss_total / count).reshape(1)
    return (
        grad_field.astype(jnp.bfloat16),
        conv_grad,
        conv_bias_grad,
        head_grad,
        head_bias_grad,
        loss,
    )


def solution(mesh):
    return jax.shard_map(
        per_device,
        mesh=mesh,
        in_specs=(
            P(None, ("parts", "row"), "col"),
            P(("parts", "row", "col"), None),
            P("parts"),
            P(),
            P(),
            P(),
            P(),
        ),
        out_specs=(
            P(None, ("parts", "row"), "col"),
            P("parts", None, None, None),
            P("parts"),
            P("parts", None),
            P("parts"),
            P("parts"),
        ),
        check_vma=False,
    )
```

profile of v0, /device:TPU:0, one launch (start us, length us, event | category | flops | bytes accessed | tf_op | source)
XLA Modules:
  0.0 410.8 jit_solution(8611053157606536604)
XLA Ops:
  13.8 4.4 %fusion.60 = f32[64,64,256]{2,0,1:T(8,128)} fusion(bf16[3,3,64,64]{3,2,1,0:T(8,128)(2,1)} %param.10, bf16[64,64,256]{2,1,0:T(8,128)(2,1)S(1)} %copy-done.10), kind=kOutput, calls=%fused_computation.100 | convolution fusion | flops 134217728 | bytes 6307840 | tf_op jit(solution)/shard_map/oc,cij->oij/dot_general | solution.py:68
  25.1 4.9 %collective-permute-start.2 = (bf16[64,72,4]{1,0,2:T(8,128)(2,1)}, bf16[64,72,4]{1,0,2:T(8,128)(2,1)}, u32[]{:S(2)}, u32[]{:S(2)}) collective-permute-start(bf16[64,72,4]{1,0,2:T(8,128)(2,1)} %copy.58), channel_id=1, source_target_pairs={{0,1},{2,3},{4,5},{6,7},{8,9},{10,11},{12,13},{14,15},{16,17},{18,... | collective-permute-start | bytes 110600 | tf_op jit(solution)/shard_map/ppermute | solution.py:17
  33.7 4.3 %fusion.41 = f32[64,256,64]{1,2,0:T(8,128)} fusion(bf16[64,64,256]{2,0,1:T(8,128)(2,1)} %copy-done.7, bf16[64,4,256]{2,0,1:T(8,128)(2,1)} %copy-done.23, bf16[3,3,64,64]{3,2,1,0:T(8,128)(2,1)} %param.10), kind=kOutput, calls=%fused_computation.67 | convolution fusion | flops 138412032 | bytes 6438912 | tf_op jit(solution)/shard_map/oc,cij->oij/dot_general | solution.py:68
  58.1 3.9 fusion.56
  65.9 13.3 %fusion = (bf16[64,64,256]{2,0,1:T(8,128)(2,1)S(1)}, f32[64,64,256]{2,0,1:T(8,128)}) fusion(bf16[64,72,4]{2,0,1:T(8,128)(2,1)S(1)} %copy.62, bf16[64,72,256]{2,0,1:T(8,128)(2,1)S(1)} %constant_dynamic-update-slice_fusion, bf16[3,3,64,64]{3,2,1,0:T(8,128)(2,1)} %param.10, f32[64,256,64]{1,2,0:T(8,128)} %fusion.43, f32[64,256,64]{1,2,0:T(8,128)} %fusion.47, ...), kind=kOutput, calls=%fused_computation.6 | convolution fusion | flops 152043520 | bytes 42258688 | tf_op jit(solution)/shard_map/oc,cij->oij/dot_general | solution.py:68
  80.4 29.7 %all_to_all.35 = bf16[64,2,32,256]{3,2,0,1:T(8,128)(2,1)} all-to-all(bf16[64,2,32,256]{3,2,0,1:T(8,128)(2,1)S(1)} %copy.65), channel_id=1, replica_groups=mesh['parts'=2,'row'=8,'col'=2] {'col'}, dimensions={1} | all-to-all | bytes 4194304 | tf_op jit(solution)/shard_map/all_to_all | solution.py:30
  110.1 5.0 %copy.66 = bf16[64,2,32,256]{0,3,1,2:T(8,128)(2,1)} copy(bf16[64,2,32,256]{3,2,0,1:T(8,128)(2,1)} %all_to_all.35) | data formatting | bytes 4194304 | tf_op jit(solution)/shard_map/all_to_all | solution.py:30
  115.0 5.3 %copy.126 = bf16[64,32,16,32]{0,3,1,2:T(8,128)(2,1)} copy(bf16[64,32,16,32]{0,3,2,1:T(8,128)(2,1)} %bitcast.202) | data formatting | bytes 4194304 | tf_op jit(solution)/shard_map/reshape;reshape | solution.py:49
  120.3 7.5 %reshape.99 = bf16[16,2,32768]{2,1,0:T(2,128)(2,1)} reshape(bf16[16,32,32,64]{3,2,1,0:T(8,128)(2,1)} %bitcast.205) | data formatting | bytes 4194304
  127.9 6.9 %all-to-all-start.1 = ((bf16[16,2,32768]{2,1,0:T(2,128)(2,1)}), bf16[16,2,32768]{2,1,0:T(2,128)(2,1)}, u32[]{:S(2)}, u32[]{:S(2)}) async-start(bf16[16,2,32768]{2,1,0:T(2,128)(2,1)} %reshape.99), calls=%async_computation.1 | async-start | bytes 4194304 | tf_op jit(solution)/shard_map/all_to_all | solution.py:50
  136.7 6.1 %fusion.93 = f32[32,512,37]{1,2,0:T(8,128)} fusion(bf16[64,32,512]{0,2,1:T(8,128)(2,1)} %bitcast.203, bf16[37,64]{1,0:T(8,128)(2,1)S(1)} %copy-done), kind=kOutput, calls=%fused_computation.133 | convolution fusion | flops 77594624 | bytes 4526720 | tf_op jit(solution)/shard_map/kc,cij->kij/dot_general | solution.py:80
  142.9 34.0 %all-to-all-done.1 = bf16[16,2,32768]{2,1,0:T(2,128)(2,1)} async-done(((bf16[16,2,32768]{2,1,0:T(2,128)(2,1)}), bf16[16,2,32768]{2,1,0:T(2,128)(2,1)}, u32[]{:S(2)}, u32[]{:S(2)}) %all-to-all-start.1) | async-done | bytes 2097184 | tf_op jit(solution)/shard_map/all_to_all | solution.py:50
  176.9 7.4 %reshape.100 = bf16[16,32,32,64]{3,2,1,0:T(8,128)(2,1)} reshape(bf16[16,2,32768]{2,1,0:T(2,128)(2,1)} %all-to-all-done.1) | data formatting | bytes 4194304
  184.3 7.9 %fusion.10 = (f32[32,512]{1,0:T(8,128)S(1)}, f32[32,512]{1,0:T(8,128)S(1)}, f32[32,512,37]{1,2,0:T(8,128)S(1)}) fusion(s32[32,512]{1,0:T(8,128)} %param.8, f32[37]{0:T(128)} %param.13, f32[32,512,37]{1,2,0:T(8,128)} %fusion.93, bf16[37,64]{1,0:T(8,128)(2,1)S(1)} %copy-done, bf16[64,32,512]{0,1,2:T(8,128)(2,1)} %bitcast.207), kind=kOutput, calls=%fused_computation.32 | convolution fusion | flops 81805312 | bytes 7148308 | tf_op jit(solution)/shard_map/kc,cij->kij/dot_general | solution.py:81
  201.5 4.5 %all-to-all-start.2 = ((bf16[37,32,2,256]{3,1,0,2:T(8,128)(2,1)}), bf16[37,32,2,256]{3,1,0,2:T(8,128)(2,1)}, u32[]{:S(2)}, u32[]{:S(2)}) async-start(bf16[37,32,2,256]{3,1,0,2:T(8,128)(2,1)} %copy.72), calls=%async_computation.2 | async-start | bytes 2424832 | tf_op jit(solution)/shard_map/all_to_all | solution.py:38
  206.2 4.1 convolution_bitcast_fusion.7
  210.3 10.8 %all-to-all-done.2 = bf16[37,32,2,256]{3,1,0,2:T(8,128)(2,1)} async-done(((bf16[37,32,2,256]{3,1,0,2:T(8,128)(2,1)}), bf16[37,32,2,256]{3,1,0,2:T(8,128)(2,1)}, u32[]{:S(2)}, u32[]{:S(2)}) %all-to-all-start.2) | async-done | bytes 1212448 | tf_op jit(solution)/shard_map/all_to_all | solution.py:38
  223.1 4.2 %convert_reduce_fusion = (f32[64]{0:T(128)}, bf16[64,64,256]{2,0,1:T(8,128)(2,1)S(1)}) fusion(f32[64,64,256]{2,0,1:T(8,128)} %get-tuple-element.45, bf16[37,64,256]{2,0,1:T(8,128)(2,1)S(1)} %bitcast.208, bf16[37,64]{1,0:T(8,128)(2,1)S(1)} %copy-done), kind=kOutput, calls=%fused_computation.17 | convolution fusion | flops 84934592 | bytes 7508864 | tf_op jit(solution)/shard_map/kc,kij->cij/dot_general | solution.py:99
  243.0 4.4 %collective-permute-start.4 = (bf16[64,4,256]{2,0,1:T(8,128)(2,1)S(1)}, bf16[64,4,256]{2,0,1:T(8,128)(2,1)S(1)}, u32[]{:S(2)}, u32[]{:S(2)}) collective-permute-start(bf16[64,4,256]{2,0,1:T(8,128)(2,1)S(1)} %get-tuple-element.39), channel_id=1, source_target_pairs={{0,2},{2,4},{4,6},{6,8},{8,10},{10,12},{12,14},{1,3},{3,5},{5,7},{... | collective-permute-start | bytes 393224 | tf_op jit(solution)/shard_map/ppermute | solution.py:17
  249.0 62.7 %all-reduce = (f32[64]{0:T(128)}, f32[37,64]{1,0:T(8,128)}, f32[37]{0:T(128)}, f32[]{:T(128)}) all-reduce(f32[64]{0:T(128)S(1)} %copy-done.30, f32[37,64]{1,0:T(8,128)S(1)} %copy-done.26, f32[37]{0:T(128)S(1)} %get-tuple-element.30, f32[]{:T(128)} %get-tuple-element.42), channel_id=1, replica_groups=mesh['parts'=2,'row'=8,'col'=2] {'row','col'}, use_global_device_ids=true, to_apply=%region_3.4 | all-reduce | flops 2470 | bytes 19760 | tf_op jit(solution)/shard_map/psum | solution.py:135
  324.1 5.9 %collective-permute-start.7 = (bf16[64,72,4]{1,0,2:T(8,128)(2,1)}, bf16[64,72,4]{1,0,2:T(8,128)(2,1)}, u32[]{:S(2)}, u32[]{:S(2)}) collective-permute-start(bf16[64,72,4]{1,0,2:T(8,128)(2,1)} %copy.78), channel_id=1, source_target_pairs={{0,1},{2,3},{4,5},{6,7},{8,9},{10,11},{12,13},{14,15},{16,17},{18,... | collective-permute-start | bytes 110600 | tf_op jit(solution)/shard_map/ppermute | solution.py:17
  343.5 6.5 %maximum_maximum_fusion = (bf16[64,72,260]{2,0,1:T(8,128)(2,1)S(1)}, bf16[64,72,260]{2,0,1:T(8,128)(2,1)S(1)}) fusion(bf16[64,4,256]{2,0,1:T(8,128)(2,1)S(1)} %copy-done.16, bf16[64,64,256]{2,0,1:T(8,128)(2,1)S(1)} %copy-done.3, bf16[64,4,256]{2,0,1:T(8,128)(2,1)S(1)} %copy-done.18, bf16[64,72,4]{2,0,1:T(8,128)(2,1)} %copy.79, bf16[64,72,4]{2,0,1:T(8,128)(2,1)S(1)} %copy.75), kind=kLoop, calls=%fused_computation.23 | loop fusion | flops 19169280 | bytes 7225344 | tf_op jit(solution)/shard_map/concatenate | solution.py:15
  364.3 10.8 %fusion.24 = bf16[64,64,256]{2,0,1:T(8,128)(2,1)S(1)} fusion(f32[64,256,64]{1,2,0:T(8,128)} %fusion.16, f32[64,256,64]{1,2,0:T(8,128)} %fusion.29, f32[64,256,64]{1,2,0:T(8,128)} %fusion.31, f32[64,256,64]{1,2,0:T(8,128)S(1)} %copy-done.12, f32[64,256,64]{1,2,0:T(8,128)} %fusion.33, f32[64,256,64]{1,2,0:T(8,128)} %fusion.35, f32[64,256,64]{1,2,0:T(8,128)} %fusion.37, ...), kind=kOutput, calls=%fused_computation.50 | convolution fusion | flops 143654912 | bytes 37765120 | tf_op jit(solution)/shard_map/oc,oij->cij/dot_general | solution.py:126
  377.5 23.2 %all-reduce.3.cloned.1.call-done = f32[3,3,64,64]{3,2,1,0:T(8,128)} async-done(((f32[3,3,64,64]{3,2,1,0:T(8,128)}), f32[3,3,64,64]{3,2,1,0:T(8,128)}) %all-reduce.3.cloned.1.call-update) | async-done | bytes 147472 | tf_op jit(solution)/shard_map/psum | solution.py:135
  (132 shorter events, 115.8 us)
Async XLA Ops:
  7.2 129.6 %copy-start = (bf16[37,64]{1,0:T(8,128)(2,1)S(1)}, bf16[37,64]{1,0:T(8,128)(2,1)}, u32[]{:S(2)}) copy-start(bf16[37,64]{1,0:T(8,128)(2,1)} %param.12) | copy-start | bytes 14212
  7.2 6.6 %copy-start.10 = (bf16[64,64,256]{2,1,0:T(8,128)(2,1)S(1)}, bf16[64,64,256]{2,1,0:T(8,128)(2,1)}, u32[]{:S(2)}) copy-start(bf16[64,64,256]{2,1,0:T(8,128)(2,1)} %param.7) | copy-start | bytes 6291460
  10.1 8.1 %copy-start.7 = (bf16[64,64,256]{2,0,1:T(8,128)(2,1)}, bf16[64,64,256]{2,0,1:T(8,128)(2,1)S(1)}, u32[]{:S(2)}) copy-start(bf16[64,64,256]{2,0,1:T(8,128)(2,1)S(1)} %copy.55) | copy-start | bytes 6291460
  10.2 8.1 %collective-permute-start = (bf16[64,4,256]{2,0,1:T(8,128)(2,1)S(1)}, bf16[64,4,256]{2,0,1:T(8,128)(2,1)S(1)}, u32[]{:S(2)}, u32[]{:S(2)}) collective-permute-start(bf16[64,4,256]{2,0,1:T(8,128)(2,1)S(1)} %get-tuple-element.40), channel_id=1, source_target_pairs={{0,2},{2,4},{4,6},{6,8},{8,10},{10,12},{12,14},{1,3},{3,5},{5,7},{... | collective-permute-start | bytes 393224 | tf_op jit(solution)/shard_map/ppermute | solution.py:17
  12.5 6.9 %collective-permute-start.1 = (bf16[64,4,256]{2,0,1:T(8,128)(2,1)S(1)}, bf16[64,4,256]{2,0,1:T(8,128)(2,1)S(1)}, u32[]{:S(2)}, u32[]{:S(2)}) collective-permute-start(bf16[64,4,256]{2,0,1:T(8,128)(2,1)S(1)} %get-tuple-element.41), channel_id=1, source_target_pairs={{2,0},{4,2},{6,4},{8,6},{10,8},{12,10},{14,12},{3,1},{5,3},{7,5},{... | collective-permute-start | bytes 393224 | tf_op jit(solution)/shard_map/ppermute | solution.py:19
  25.1 16.2 %collective-permute-start.2 = (bf16[64,72,4]{1,0,2:T(8,128)(2,1)}, bf16[64,72,4]{1,0,2:T(8,128)(2,1)}, u32[]{:S(2)}, u32[]{:S(2)}) collective-permute-start(bf16[64,72,4]{1,0,2:T(8,128)(2,1)} %copy.58), channel_id=1, source_target_pairs={{0,1},{2,3},{4,5},{6,7},{8,9},{10,11},{12,13},{14,15},{16,17},{18,... | collective-permute-start | bytes 110600 | tf_op jit(solution)/shard_map/ppermute | solution.py:17
  32.0 19.4 %collective-permute-start.3 = (bf16[64,72,4]{1,0,2:T(8,128)(2,1)}, bf16[64,72,4]{1,0,2:T(8,128)(2,1)}, u32[]{:S(2)}, u32[]{:S(2)}) collective-permute-start(bf16[64,72,4]{1,0,2:T(8,128)(2,1)} %copy.61), channel_id=1, source_target_pairs={{1,0},{3,2},{5,4},{7,6},{9,8},{11,10},{13,12},{15,14},{17,16},{19,... | collective-permute-start | bytes 110600 | tf_op jit(solution)/shard_map/ppermute | solution.py:19
  127.9 49.0 %all-to-all-start.1 = ((bf16[16,2,32768]{2,1,0:T(2,128)(2,1)}), bf16[16,2,32768]{2,1,0:T(2,128)(2,1)}, u32[]{:S(2)}, u32[]{:S(2)}) async-start(bf16[16,2,32768]{2,1,0:T(2,128)(2,1)} %reshape.99), calls=%async_computation.1 | async-start | bytes 4194304 | tf_op jit(solution)/shard_map/all_to_all | solution.py:50
  184.3 7.9 %copy-start.29 = (pred[32]{0:T(512)(128)(4,1)S(1)}, pred[32]{0:T(512)(128)(4,1)}, u32[]{:S(2)}) copy-start(pred[32]{0:T(512)(128)(4,1)} %copy-done.28) | copy-start | bytes 100
  184.3 8.6 %copy-start.25 = (f32[32,512]{1,0:T(8,128)S(1)}, f32[32,512]{1,0:T(8,128)}, u32[]{:S(2)}) copy-start(f32[32,512]{1,0:T(8,128)} %and_convert_fusion) | copy-start | bytes 196612
  184.3 8.6 %copy-start.27 = (s32[32,512]{1,0:T(8,128)S(1)}, s32[32,512]{1,0:T(8,128)}, u32[]{:S(2)}) copy-start(s32[32,512]{1,0:T(8,128)} %param.8) | copy-start | bytes 196612
  201.5 19.6 %all-to-all-start.2 = ((bf16[37,32,2,256]{3,1,0,2:T(8,128)(2,1)}), bf16[37,32,2,256]{3,1,0,2:T(8,128)(2,1)}, u32[]{:S(2)}, u32[]{:S(2)}) async-start(bf16[37,32,2,256]{3,1,0,2:T(8,128)(2,1)} %copy.72), calls=%async_computation.2 | async-start | bytes 2424832 | tf_op jit(solution)/shard_map/all_to_all | solution.py:38
  206.0 194.7 %all-reduce.3.cloned.1.call-start = ((), (), s32[]{:S(2)}) async-start(), calls=%async_computation.3 | async-start | bytes 589824 | tf_op jit(solution)/shard_map/psum | solution.py:135
  227.3 20.9 %copy-start.2 = (bf16[64,64,256]{2,0,1:T(8,128)(2,1)}, bf16[64,64,256]{2,0,1:T(8,128)(2,1)S(1)}, u32[]{:S(2)}) copy-start(bf16[64,64,256]{2,0,1:T(8,128)(2,1)S(1)} %get-tuple-element.48) | copy-start | bytes 6291460
  238.1 9.4 %copy-start.9 = (bf16[64,64,256]{2,0,1:T(8,128)(2,1)S(1)}, bf16[64,64,256]{2,0,1:T(8,128)(2,1)}, u32[]{:S(2)}) copy-start(bf16[64,64,256]{2,0,1:T(8,128)(2,1)} %copy-done.7) | copy-start | bytes 6291460
  238.1 9.4 %copy-start.24 = (bf16[64,4,256]{2,0,1:T(8,128)(2,1)S(1)}, bf16[64,4,256]{2,0,1:T(8,128)(2,1)}, u32[]{:S(2)}) copy-start(bf16[64,4,256]{2,0,1:T(8,128)(2,1)} %copy-done.23) | copy-start | bytes 393220
  241.7 71.4 %collective-permute-start.5 = (bf16[64,4,256]{2,0,1:T(8,128)(2,1)S(1)}, bf16[64,4,256]{2,0,1:T(8,128)(2,1)S(1)}, u32[]{:S(2)}, u32[]{:S(2)}) collective-permute-start(bf16[64,4,256]{2,0,1:T(8,128)(2,1)S(1)} %get-tuple-element.38), channel_id=1, source_target_pairs={{2,0},{4,2},{6,4},{8,6},{10,8},{12,10},{14,12},{3,1},{5,3},{7,5},{... | collective-permute-start | bytes 393224 | tf_op jit(solution)/shard_map/ppermute | solution.py:19
  243.0 70.1 %collective-permute-start.4 = (bf16[64,4,256]{2,0,1:T(8,128)(2,1)S(1)}, bf16[64,4,256]{2,0,1:T(8,128)(2,1)S(1)}, u32[]{:S(2)}, u32[]{:S(2)}) collective-permute-start(bf16[64,4,256]{2,0,1:T(8,128)(2,1)S(1)} %get-tuple-element.39), channel_id=1, source_target_pairs={{0,2},{2,4},{4,6},{6,8},{8,10},{10,12},{12,14},{1,3},{3,5},{5,7},{... | collective-permute-start | bytes 393224 | tf_op jit(solution)/shard_map/ppermute | solution.py:17
  318.0 12.0 %copy-start.3 = (bf16[64,64,256]{2,0,1:T(8,128)(2,1)S(1)}, bf16[64,64,256]{2,0,1:T(8,128)(2,1)}, u32[]{:S(2)}) copy-start(bf16[64,64,256]{2,0,1:T(8,128)(2,1)} %copy-done.2) | copy-start | bytes 6291460
  318.0 12.0 %copy-start.15 = (bf16[64,4,256]{2,0,1:T(8,128)(2,1)S(1)}, bf16[64,4,256]{2,0,1:T(8,128)(2,1)}, u32[]{:S(2)}) copy-start(bf16[64,4,256]{2,0,1:T(8,128)(2,1)} %copy-done.14) | copy-start | bytes 393220
  320.8 16.2 %collective-permute-start.6 = (bf16[64,72,4]{1,0,2:T(8,128)(2,1)S(1)}, bf16[64,72,4]{1,0,2:T(8,128)(2,1)}, u32[]{:S(2)}, u32[]{:S(2)}) collective-permute-start(bf16[64,72,4]{1,0,2:T(8,128)(2,1)S(1)} %copy.74), channel_id=1, source_target_pairs={{1,0},{3,2},{5,4},{7,6},{9,8},{11,10},{13,12},{15,14},{17,16},{19,... | collective-permute-start | bytes 110600 | tf_op jit(solution)/shard_map/ppermute | solution.py:19
  324.1 9.4 %copy-start.18 = (bf16[64,4,256]{2,0,1:T(8,128)(2,1)S(1)}, bf16[64,4,256]{2,0,1:T(8,128)(2,1)}, u32[]{:S(2)}) copy-start(bf16[64,4,256]{2,0,1:T(8,128)(2,1)} %copy-done.17) | copy-start | bytes 393220
  324.1 15.7 %collective-permute-start.7 = (bf16[64,72,4]{1,0,2:T(8,128)(2,1)}, bf16[64,72,4]{1,0,2:T(8,128)(2,1)}, u32[]{:S(2)}, u32[]{:S(2)}) collective-permute-start(bf16[64,72,4]{1,0,2:T(8,128)(2,1)} %copy.78), channel_id=1, source_target_pairs={{0,1},{2,3},{4,5},{6,7},{8,9},{10,11},{12,13},{14,15},{16,17},{18,... | collective-permute-start | bytes 110600 | tf_op jit(solution)/shard_map/ppermute | solution.py:17
  364.3 38.2 %copy-start.1 = (bf16[37,64]{1,0:T(8,128)(2,1)S(1)}, bf16[37,64]{1,0:T(8,128)(2,1)}, u32[]{:S(2)}) copy-start(bf16[37,64]{1,0:T(8,128)(2,1)} %param.12) | copy-start | bytes 14212
  (19 other events, 57.2 us)
Sparse Core Ops, SparseCore 0:
  313.2 87.4 all-reduce.2
where the time goes:
time: 418 us; the launch traced here: 411 us
  matrix products  113 us (27%)
  blocking collectives  92.3 us (22%)
  local copies, waits for them, and re-layouts  72.9 us (17%)
  waiting for transfers between devices  68.1 us (16%)
  starting transfers between devices  34.7 us (8%)
  between operations  17.4 us (4%)
  other arithmetic  12.7 us (3%)
    psum x1, blocking collectives, per_device(): lax.psum((conv_grad, conv_bias_grad, head_grad, head_bias_grad, loss_loca...  62.7 us
    dot_general x9, matrix products, per_device(): jnp.einsum('oc,cij->oij', conv_weight[offset_row, offset_column], sliding...  44.2 us
    dot_general x9, matrix products, per_device(): jnp.einsum('oc,oij->cij', conv_weight[offset_row, offset_column], source,...  35.5 us
    all_to_all x1, waiting for transfers between devices, mirror_features(): lax.all_to_all(blocks, ('row', 'col'), split_axis=2, concat_axis=2, tiled...  34 us
    all_to_all x1, blocking collectives, tile_to_band(): lax.all_to_all(split, 'col', split_axis=1, concat_axis=3, tiled=True)  29.7 us
    unnamed x71, local copies, waits for them, and re-layouts  27.2 us
    psum x1, waiting for transfers between devices, per_device(): lax.psum((conv_grad, conv_bias_grad, head_grad, head_bias_grad, loss_loca...  23.2 us
    ppermute x4, starting transfers between devices, with_halo(): lax.ppermute(tail, axis, [(i, (i + 1) % count) for i in range(ends)])  17.6 us
  transfers between devices with their start and end apart: 11, of which 3 were waited for; matrix products, arithmetic and copies ran while one was open for 23% of the time, Pallas kernels for 0%

commit v1 on v0

--- a/solution.py
+++ b/solution.py
@@ -133,7 +133,7 @@
     conv_grad = jnp.stack(tap_rows)
     conv_bias_grad = jnp.sum(preact_gradient.astype(jnp.float32), axis=(1, 2))
     conv_grad, conv_bias_grad, head_grad, head_bias_grad, loss_total = lax.psum(
-        (conv_grad, conv_bias_grad, head_grad, head_bias_grad, loss_local), ("row", "col")
+        lax.psum((conv_grad, conv_bias_grad, head_grad, head_bias_grad, loss_local), "col"), "row"
     )
     loss = (loss_total / count).reshape(1)
     return (

time: 418 us -> 386 us (0.923)
  the two profiles are of different devices: /device:TPU:0 before, /device:TPU:1 now
where the time goes in v1:
time: 386 us; the launch traced here: 379 us
  matrix products  113 us (29%)
  local copies, waits for them, and re-layouts  72.2 us (19%)
  waiting for transfers between devices  65.8 us (17%)
  blocking collectives  58.7 us (15%)
  starting transfers between devices  39 us (10%)
  between operations  17.4 us (5%)
  other arithmetic  12.7 us (3%)
    dot_general x9, matrix products, per_device(): jnp.einsum('oc,cij->oij', conv_weight[offset_row, offset_column], sliding...  44.2 us
    all_to_all x1, waiting for transfers between devices, mirror_features(): lax.all_to_all(blocks, ('row', 'col'), split_axis=2, concat_axis=2, tiled...  36.1 us
    dot_general x9, matrix products, per_device(): jnp.einsum('oc,oij->cij', conv_weight[offset_row, offset_column], source,...  35.5 us
    all_to_all x1, blocking collectives, tile_to_band(): lax.all_to_all(split, 'col', split_axis=1, concat_axis=3, tiled=True)  28.5 us
    unnamed x61, local copies, waits for them, and re-layouts  26 us
    psum x1, blocking collectives, per_device(): lax.psum(lax.psum((conv_grad, conv_bias_grad, head_grad, head_bias_grad,...  24 us
    ppermute x4, starting transfers between devices, with_halo(): lax.ppermute(tail, axis, [(i, (i + 1) % count) for i in range(ends)])  21.1 us
    psum x1, waiting for transfers between devices, per_device(): lax.psum(lax.psum((conv_grad, conv_bias_grad, head_grad, head_bias_grad,...  15.7 us
  transfers between devices with their start and end apart: 12, of which 4 were waited for; matrix products, arithmetic and copies ran while one was open for 25% of the time, Pallas kernels for 0%

profile of v1, /device:TPU:1, one launch (start us, length us, event | category | flops | bytes accessed | tf_op | source)
XLA Modules:
  0.0 378.6 jit_solution(1891917622029278764)
XLA Ops:
  10.2 4.6 %collective-permute-start = (bf16[64,4,256]{2,0,1:T(8,128)(2,1)S(1)}, bf16[64,4,256]{2,0,1:T(8,128)(2,1)S(1)}, u32[]{:S(2)}, u32[]{:S(2)}) collective-permute-start(bf16[64,4,256]{2,0,1:T(8,128)(2,1)S(1)} %get-tuple-element.44), channel_id=1, source_target_pairs={{0,2},{2,4},{4,6},{6,8},{8,10},{10,12},{12,14},{1,3},{3,5},{5,7},{... | collective-permute-start | bytes 393224 | tf_op jit(solution)/shard_map/ppermute | solution.py:17
  16.7 4.4 %fusion.60 = f32[64,64,256]{2,0,1:T(8,128)} fusion(bf16[3,3,64,64]{3,2,1,0:T(8,128)(2,1)} %param.10, bf16[64,64,256]{2,1,0:T(8,128)(2,1)S(1)} %copy-done.10), kind=kOutput, calls=%fused_computation.100 | convolution fusion | flops 134217728 | bytes 6307840 | tf_op jit(solution)/shard_map/oc,cij->oij/dot_general | solution.py:68
  35.3 4.3 %fusion.41 = f32[64,256,64]{1,2,0:T(8,128)} fusion(bf16[64,64,256]{2,0,1:T(8,128)(2,1)} %copy-done.7, bf16[64,4,256]{2,0,1:T(8,128)(2,1)} %copy-done.18, bf16[3,3,64,64]{3,2,1,0:T(8,128)(2,1)} %param.10), kind=kOutput, calls=%fused_computation.67 | convolution fusion | flops 138412032 | bytes 6438912 | tf_op jit(solution)/shard_map/oc,cij->oij/dot_general | solution.py:68
  67.6 13.3 %fusion = (bf16[64,64,256]{2,0,1:T(8,128)(2,1)S(1)}, f32[64,64,256]{2,0,1:T(8,128)}) fusion(bf16[64,72,4]{2,0,1:T(8,128)(2,1)S(1)} %copy.62, bf16[64,72,256]{2,0,1:T(8,128)(2,1)S(1)} %constant_dynamic-update-slice_fusion, bf16[3,3,64,64]{3,2,1,0:T(8,128)(2,1)} %param.10, f32[64,256,64]{1,2,0:T(8,128)} %fusion.43, f32[64,256,64]{1,2,0:T(8,128)} %fusion.47, ...), kind=kOutput, calls=%fused_computation.6 | convolution fusion | flops 152043520 | bytes 42258688 | tf_op jit(solution)/shard_map/oc,cij->oij/dot_general | solution.py:68
  82.1 28.5 %all_to_all.35 = bf16[64,2,32,256]{3,2,0,1:T(8,128)(2,1)} all-to-all(bf16[64,2,32,256]{3,2,0,1:T(8,128)(2,1)S(1)} %copy.65), channel_id=1, replica_groups=mesh['parts'=2,'row'=8,'col'=2] {'col'}, dimensions={1} | all-to-all | bytes 4194304 | tf_op jit(solution)/shard_map/all_to_all | solution.py:30
  110.6 5.0 %copy.66 = bf16[64,2,32,256]{0,3,1,2:T(8,128)(2,1)} copy(bf16[64,2,32,256]{3,2,0,1:T(8,128)(2,1)} %all_to_all.35) | data formatting | bytes 4194304 | tf_op jit(solution)/shard_map/all_to_all | solution.py:30
  115.6 5.3 %copy.126 = bf16[64,32,16,32]{0,3,1,2:T(8,128)(2,1)} copy(bf16[64,32,16,32]{0,3,2,1:T(8,128)(2,1)} %bitcast.202) | data formatting | bytes 4194304 | tf_op jit(solution)/shard_map/reshape;reshape | solution.py:49
  120.9 7.6 %reshape.99 = bf16[16,2,32768]{2,1,0:T(2,128)(2,1)} reshape(bf16[16,32,32,64]{3,2,1,0:T(8,128)(2,1)} %bitcast.205) | data formatting | bytes 4194304
  128.4 6.4 %all-to-all-start.1 = ((bf16[16,2,32768]{2,1,0:T(2,128)(2,1)}), bf16[16,2,32768]{2,1,0:T(2,128)(2,1)}, u32[]{:S(2)}, u32[]{:S(2)}) async-start(bf16[16,2,32768]{2,1,0:T(2,128)(2,1)} %reshape.99), calls=%async_computation.1 | async-start | bytes 4194304 | tf_op jit(solution)/shard_map/all_to_all | solution.py:50
  136.7 6.1 %fusion.93 = f32[32,512,37]{1,2,0:T(8,128)} fusion(bf16[64,32,512]{0,2,1:T(8,128)(2,1)} %bitcast.203, bf16[37,64]{1,0:T(8,128)(2,1)S(1)} %copy-done), kind=kOutput, calls=%fused_computation.133 | convolution fusion | flops 77594624 | bytes 4526720 | tf_op jit(solution)/shard_map/kc,cij->kij/dot_general | solution.py:80
  142.9 36.1 %all-to-all-done.1 = bf16[16,2,32768]{2,1,0:T(2,128)(2,1)} async-done(((bf16[16,2,32768]{2,1,0:T(2,128)(2,1)}), bf16[16,2,32768]{2,1,0:T(2,128)(2,1)}, u32[]{:S(2)}, u32[]{:S(2)}) %all-to-all-start.1) | async-done | bytes 2097184 | tf_op jit(solution)/shard_map/all_to_all | solution.py:50
  179.0 7.5 %reshape.100 = bf16[16,32,32,64]{3,2,1,0:T(8,128)(2,1)} reshape(bf16[16,2,32768]{2,1,0:T(2,128)(2,1)} %all-to-all-done.1) | data formatting | bytes 4194304
  186.5 7.9 %fusion.10 = (f32[32,512]{1,0:T(8,128)S(1)}, f32[32,512]{1,0:T(8,128)S(1)}, f32[32,512,37]{1,2,0:T(8,128)S(1)}) fusion(s32[32,512]{1,0:T(8,128)} %param.8, f32[37]{0:T(128)} %param.13, f32[32,512,37]{1,2,0:T(8,128)} %fusion.93, bf16[37,64]{1,0:T(8,128)(2,1)S(1)} %copy-done, bf16[64,32,512]{0,1,2:T(8,128)(2,1)} %bitcast.207), kind=kOutput, calls=%fused_computation.32 | convolution fusion | flops 81805312 | bytes 7148308 | tf_op jit(solution)/shard_map/kc,cij->kij/dot_general | solution.py:81
  203.7 4.5 %all-to-all-start.2 = ((bf16[37,32,2,256]{3,1,0,2:T(8,128)(2,1)}), bf16[37,32,2,256]{3,1,0,2:T(8,128)(2,1)}, u32[]{:S(2)}, u32[]{:S(2)}) async-start(bf16[37,32,2,256]{3,1,0,2:T(8,128)(2,1)} %copy.72), calls=%async_computation.2 | async-start | bytes 2424832 | tf_op jit(solution)/shard_map/all_to_all | solution.py:38
  212.4 9.8 %all-to-all-done.2 = bf16[37,32,2,256]{3,1,0,2:T(8,128)(2,1)} async-done(((bf16[37,32,2,256]{3,1,0,2:T(8,128)(2,1)}), bf16[37,32,2,256]{3,1,0,2:T(8,128)(2,1)}, u32[]{:S(2)}, u32[]{:S(2)}) %all-to-all-start.2) | async-done | bytes 1212448 | tf_op jit(solution)/shard_map/all_to_all | solution.py:38
  224.2 4.2 %convert_reduce_fusion = (f32[64]{0:T(128)}, bf16[64,64,256]{2,0,1:T(8,128)(2,1)S(1)}) fusion(f32[64,64,256]{2,0,1:T(8,128)} %get-tuple-element.49, bf16[37,64,256]{2,0,1:T(8,128)(2,1)S(1)} %bitcast.208, bf16[37,64]{1,0:T(8,128)(2,1)S(1)} %copy-done), kind=kOutput, calls=%fused_computation.17 | convolution fusion | flops 84934592 | bytes 7508864 | tf_op jit(solution)/shard_map/kc,kij->cij/dot_general | solution.py:99
  244.7 7.5 %collective-permute-start.4 = (bf16[64,4,256]{2,0,1:T(8,128)(2,1)S(1)}, bf16[64,4,256]{2,0,1:T(8,128)(2,1)S(1)}, u32[]{:S(2)}, u32[]{:S(2)}) collective-permute-start(bf16[64,4,256]{2,0,1:T(8,128)(2,1)S(1)} %get-tuple-element.43), channel_id=1, source_target_pairs={{0,2},{2,4},{4,6},{6,8},{8,10},{10,12},{12,14},{1,3},{3,5},{5,7},{... | collective-permute-start | bytes 393224 | tf_op jit(solution)/shard_map/ppermute | solution.py:17
  253.8 6.2 %all-reduce.1 = (f32[64]{0:T(128)S(1)}, f32[37,64]{1,0:T(8,128)S(1)}, f32[37]{0:T(128)S(1)}, f32[]{:T(128)}) all-reduce(f32[64]{0:T(128)S(1)} %copy-done.25, f32[37,64]{1,0:T(8,128)S(1)} %copy-done.21, f32[37]{0:T(128)S(1)} %get-tuple-element.34, f32[]{:T(128)} %get-tuple-element.46), channel_id=1, replica_groups=mesh['parts'=2,'row'=8,'col'=2] {'col'}, use_global_device_ids=true, to_apply=%region_4.5 | all-reduce | flops 2470 | bytes 19760 | tf_op jit(solution)/shard_map/psum | solution.py:136
  259.9 24.0 %all-reduce = (f32[64]{0:T(128)}, f32[37,64]{1,0:T(8,128)}, f32[37]{0:T(128)}, f32[]{:T(128)}) all-reduce(f32[64]{0:T(128)S(1)} %get-tuple-element.30, f32[37,64]{1,0:T(8,128)S(1)} %get-tuple-element.31, f32[37]{0:T(128)S(1)} %get-tuple-element.32, f32[]{:T(128)} %get-tuple-element.33), channel_id=1, replica_groups=mesh['parts'=2,'row'=8,'col'=2] {'row'}, use_global_device_ids=true, to_apply=%region_5.6 | all-reduce | flops 2470 | bytes 19760 | tf_op jit(solution)/shard_map/psum | solution.py:135
  295.7 5.2 %collective-permute-start.7 = (bf16[64,72,4]{1,0,2:T(8,128)(2,1)}, bf16[64,72,4]{1,0,2:T(8,128)(2,1)}, u32[]{:S(2)}, u32[]{:S(2)}) collective-permute-start(bf16[64,72,4]{1,0,2:T(8,128)(2,1)} %copy.78), channel_id=1, source_target_pairs={{0,1},{2,3},{4,5},{6,7},{8,9},{10,11},{12,13},{14,15},{16,17},{18,... | collective-permute-start | bytes 110600 | tf_op jit(solution)/shard_map/ppermute | solution.py:17
  307.9 4.1 %all-reduce.5.cloned.1.call-done = f32[3,3,64,64]{3,2,1,0:T(8,128)} async-done(((f32[3,3,64,64]{3,2,1,0:T(8,128)}), f32[3,3,64,64]{3,2,1,0:T(8,128)}) %all-reduce.5.cloned.1.call-update) | async-done | bytes 147472 | tf_op jit(solution)/shard_map/psum | solution.py:136
  318.6 6.5 %maximum_maximum_fusion = (bf16[64,72,260]{2,0,1:T(8,128)(2,1)S(1)}, bf16[64,72,260]{2,0,1:T(8,128)(2,1)S(1)}) fusion(bf16[64,4,256]{2,0,1:T(8,128)(2,1)S(1)} %collective-permute-done.5, bf16[64,64,256]{2,0,1:T(8,128)(2,1)S(1)} %copy-done.3, bf16[64,4,256]{2,0,1:T(8,128)(2,1)S(1)} %collective-permute-done.4, bf16[64,72,4]{2,0,1:T(8,128)(2,1)} %copy.79, ...), kind=kLoop, calls=%fused_computation.23 | loop fusion | flops 19169280 | bytes 7225344 | tf_op jit(solution)/shard_map/concatenate | solution.py:15
  339.4 10.8 %fusion.24 = bf16[64,64,256]{2,0,1:T(8,128)(2,1)S(1)} fusion(f32[64,256,64]{1,2,0:T(8,128)} %fusion.16, f32[64,256,64]{1,2,0:T(8,128)} %fusion.29, f32[64,256,64]{1,2,0:T(8,128)} %fusion.31, f32[64,256,64]{1,2,0:T(8,128)S(1)} %copy-done.12, f32[64,256,64]{1,2,0:T(8,128)} %fusion.33, f32[64,256,64]{1,2,0:T(8,128)} %fusion.35, f32[64,256,64]{1,2,0:T(8,128)} %fusion.37, ...), kind=kOutput, calls=%fused_computation.50 | convolution fusion | flops 143654912 | bytes 37765120 | tf_op jit(solution)/shard_map/oc,oij->cij/dot_general | solution.py:126
  352.8 15.7 %all-reduce.7.cloned.1.call-done = f32[3,3,64,64]{3,2,1,0:T(8,128)} async-done(((f32[3,3,64,64]{3,2,1,0:T(8,128)}), f32[3,3,64,64]{3,2,1,0:T(8,128)}) %all-reduce.7.cloned.1.call-update) | async-done | bytes 147472 | tf_op jit(solution)/shard_map/psum | solution.py:135
  (126 shorter events, 125.8 us)
Async XLA Ops:
  7.2 129.6 %copy-start = (bf16[37,64]{1,0:T(8,128)(2,1)S(1)}, bf16[37,64]{1,0:T(8,128)(2,1)}, u32[]{:S(2)}) copy-start(bf16[37,64]{1,0:T(8,128)(2,1)} %param.12) | copy-start | bytes 14212
  7.2 9.5 %copy-start.10 = (bf16[64,64,256]{2,1,0:T(8,128)(2,1)S(1)}, bf16[64,64,256]{2,1,0:T(8,128)(2,1)}, u32[]{:S(2)}) copy-start(bf16[64,64,256]{2,1,0:T(8,128)(2,1)} %param.7) | copy-start | bytes 6291460
  10.1 11.0 %copy-start.7 = (bf16[64,64,256]{2,0,1:T(8,128)(2,1)}, bf16[64,64,256]{2,0,1:T(8,128)(2,1)S(1)}, u32[]{:S(2)}) copy-start(bf16[64,64,256]{2,0,1:T(8,128)(2,1)S(1)} %copy.55) | copy-start | bytes 6291460
  10.2 10.9 %collective-permute-start = (bf16[64,4,256]{2,0,1:T(8,128)(2,1)S(1)}, bf16[64,4,256]{2,0,1:T(8,128)(2,1)S(1)}, u32[]{:S(2)}, u32[]{:S(2)}) collective-permute-start(bf16[64,4,256]{2,0,1:T(8,128)(2,1)S(1)} %get-tuple-element.44), channel_id=1, source_target_pairs={{0,2},{2,4},{4,6},{6,8},{8,10},{10,12},{12,14},{1,3},{3,5},{5,7},{... | collective-permute-start | bytes 393224 | tf_op jit(solution)/shard_map/ppermute | solution.py:17
  14.8 8.2 %collective-permute-start.1 = (bf16[64,4,256]{2,0,1:T(8,128)(2,1)S(1)}, bf16[64,4,256]{2,0,1:T(8,128)(2,1)S(1)}, u32[]{:S(2)}, u32[]{:S(2)}) collective-permute-start(bf16[64,4,256]{2,0,1:T(8,128)(2,1)S(1)} %get-tuple-element.45), channel_id=1, source_target_pairs={{2,0},{4,2},{6,4},{8,6},{10,8},{12,10},{14,12},{3,1},{5,3},{7,5},{... | collective-permute-start | bytes 393224 | tf_op jit(solution)/shard_map/ppermute | solution.py:19
  27.9 15.1 %collective-permute-start.2 = (bf16[64,72,4]{1,0,2:T(8,128)(2,1)}, bf16[64,72,4]{1,0,2:T(8,128)(2,1)}, u32[]{:S(2)}, u32[]{:S(2)}) collective-permute-start(bf16[64,72,4]{1,0,2:T(8,128)(2,1)} %copy.58), channel_id=1, source_target_pairs={{0,1},{2,3},{4,5},{6,7},{8,9},{10,11},{12,13},{14,15},{16,17},{18,... | collective-permute-start | bytes 110600 | tf_op jit(solution)/shard_map/ppermute | solution.py:17
  33.7 19.4 %collective-permute-start.3 = (bf16[64,72,4]{1,0,2:T(8,128)(2,1)}, bf16[64,72,4]{1,0,2:T(8,128)(2,1)}, u32[]{:S(2)}, u32[]{:S(2)}) collective-permute-start(bf16[64,72,4]{1,0,2:T(8,128)(2,1)} %copy.61), channel_id=1, source_target_pairs={{1,0},{3,2},{5,4},{7,6},{9,8},{11,10},{13,12},{15,14},{17,16},{19,... | collective-permute-start | bytes 110600 | tf_op jit(solution)/shard_map/ppermute | solution.py:19
  128.4 50.6 %all-to-all-start.1 = ((bf16[16,2,32768]{2,1,0:T(2,128)(2,1)}), bf16[16,2,32768]{2,1,0:T(2,128)(2,1)}, u32[]{:S(2)}, u32[]{:S(2)}) async-start(bf16[16,2,32768]{2,1,0:T(2,128)(2,1)} %reshape.99), calls=%async_computation.1 | async-start | bytes 4194304 | tf_op jit(solution)/shard_map/all_to_all | solution.py:50
  186.5 7.9 %copy-start.24 = (pred[32]{0:T(512)(128)(4,1)S(1)}, pred[32]{0:T(512)(128)(4,1)}, u32[]{:S(2)}) copy-start(pred[32]{0:T(512)(128)(4,1)} %copy-done.23) | copy-start | bytes 100
  186.5 8.6 %copy-start.20 = (f32[32,512]{1,0:T(8,128)S(1)}, f32[32,512]{1,0:T(8,128)}, u32[]{:S(2)}) copy-start(f32[32,512]{1,0:T(8,128)} %and_convert_fusion) | copy-start | bytes 196612
  186.5 8.6 %copy-start.22 = (s32[32,512]{1,0:T(8,128)S(1)}, s32[32,512]{1,0:T(8,128)}, u32[]{:S(2)}) copy-start(s32[32,512]{1,0:T(8,128)} %param.8) | copy-start | bytes 196612
  203.7 18.5 %all-to-all-start.2 = ((bf16[37,32,2,256]{3,1,0,2:T(8,128)(2,1)}), bf16[37,32,2,256]{3,1,0,2:T(8,128)(2,1)}, u32[]{:S(2)}, u32[]{:S(2)}) async-start(bf16[37,32,2,256]{3,1,0,2:T(8,128)(2,1)} %copy.72), calls=%async_computation.2 | async-start | bytes 2424832 | tf_op jit(solution)/shard_map/all_to_all | solution.py:38
  208.2 103.9 %all-reduce.5.cloned.1.call-start = ((), (), s32[]{:S(2)}) async-start(), calls=%async_computation.3 | async-start | bytes 589824 | tf_op jit(solution)/shard_map/psum | solution.py:136
  228.4 24.6 %copy-start.2 = (bf16[64,64,256]{2,0,1:T(8,128)(2,1)}, bf16[64,64,256]{2,0,1:T(8,128)(2,1)S(1)}, u32[]{:S(2)}) copy-start(bf16[64,64,256]{2,0,1:T(8,128)(2,1)S(1)} %get-tuple-element.52) | copy-start | bytes 6291460
  239.2 13.1 %copy-start.9 = (bf16[64,64,256]{2,0,1:T(8,128)(2,1)S(1)}, bf16[64,64,256]{2,0,1:T(8,128)(2,1)}, u32[]{:S(2)}) copy-start(bf16[64,64,256]{2,0,1:T(8,128)(2,1)} %copy-done.7) | copy-start | bytes 6291460
  239.2 13.1 %copy-start.19 = (bf16[64,4,256]{2,0,1:T(8,128)(2,1)S(1)}, bf16[64,4,256]{2,0,1:T(8,128)(2,1)}, u32[]{:S(2)}) copy-start(bf16[64,4,256]{2,0,1:T(8,128)(2,1)} %copy-done.18) | copy-start | bytes 393220
  242.8 42.7 %collective-permute-start.5 = (bf16[64,4,256]{2,0,1:T(8,128)(2,1)S(1)}, bf16[64,4,256]{2,0,1:T(8,128)(2,1)S(1)}, u32[]{:S(2)}, u32[]{:S(2)}) collective-permute-start(bf16[64,4,256]{2,0,1:T(8,128)(2,1)S(1)} %get-tuple-element.42), channel_id=1, source_target_pairs={{2,0},{4,2},{6,4},{8,6},{10,8},{12,10},{14,12},{3,1},{5,3},{7,5},{... | collective-permute-start | bytes 393224 | tf_op jit(solution)/shard_map/ppermute | solution.py:19
  244.7 8.3 %copy-start.17 = (bf16[64,4,256]{2,0,1:T(8,128)(2,1)S(1)}, bf16[64,4,256]{2,0,1:T(8,128)(2,1)}, u32[]{:S(2)}) copy-start(bf16[64,4,256]{2,0,1:T(8,128)(2,1)} %copy-done.15) | copy-start | bytes 393220
  244.7 40.7 %collective-permute-start.4 = (bf16[64,4,256]{2,0,1:T(8,128)(2,1)S(1)}, bf16[64,4,256]{2,0,1:T(8,128)(2,1)S(1)}, u32[]{:S(2)}, u32[]{:S(2)}) collective-permute-start(bf16[64,4,256]{2,0,1:T(8,128)(2,1)S(1)} %get-tuple-element.43), channel_id=1, source_target_pairs={{0,2},{2,4},{4,6},{6,8},{8,10},{10,12},{12,14},{1,3},{3,5},{5,7},{... | collective-permute-start | bytes 393224 | tf_op jit(solution)/shard_map/ppermute | solution.py:17
  285.4 83.0 %all-reduce.7.cloned.1.call-start = ((), (), s32[]{:S(2)}) async-start(), calls=%async_computation.4 | async-start | bytes 589824 | tf_op jit(solution)/shard_map/psum | solution.py:135
  289.0 12.0 %copy-start.3 = (bf16[64,64,256]{2,0,1:T(8,128)(2,1)S(1)}, bf16[64,64,256]{2,0,1:T(8,128)(2,1)}, u32[]{:S(2)}) copy-start(bf16[64,64,256]{2,0,1:T(8,128)(2,1)} %copy-done.2) | copy-start | bytes 6291460
  292.4 19.6 %collective-permute-start.6 = (bf16[64,72,4]{1,0,2:T(8,128)(2,1)}, bf16[64,72,4]{1,0,2:T(8,128)(2,1)}, u32[]{:S(2)}, u32[]{:S(2)}) collective-permute-start(bf16[64,72,4]{1,0,2:T(8,128)(2,1)} %copy.74), channel_id=1, source_target_pairs={{1,0},{3,2},{5,4},{7,6},{9,8},{11,10},{13,12},{15,14},{17,16},{19,... | collective-permute-start | bytes 110600 | tf_op jit(solution)/shard_map/ppermute | solution.py:19
  295.7 19.2 %collective-permute-start.7 = (bf16[64,72,4]{1,0,2:T(8,128)(2,1)}, bf16[64,72,4]{1,0,2:T(8,128)(2,1)}, u32[]{:S(2)}, u32[]{:S(2)}) collective-permute-start(bf16[64,72,4]{1,0,2:T(8,128)(2,1)} %copy.78), channel_id=1, source_target_pairs={{0,1},{2,3},{4,5},{6,7},{8,9},{10,11},{12,13},{14,15},{16,17},{18,... | collective-permute-start | bytes 110600 | tf_op jit(solution)/shard_map/ppermute | solution.py:17
  339.4 30.7 %copy-start.1 = (bf16[37,64]{1,0:T(8,128)(2,1)S(1)}, bf16[37,64]{1,0:T(8,128)(2,1)}, u32[]{:S(2)}) copy-start(bf16[37,64]{1,0:T(8,128)(2,1)} %param.12) | copy-start | bytes 14212
  (15 other events, 44.6 us)
Sparse Core Ops, SparseCore 0:
  285.5 26.4 all-reduce.4
  314.3 54.0 all-reduce.6
